TPU v7x, 256 devices: a whole 4x4x8 slice. The times are simulated.
256 devices in a mesh: member: 8 (over x, z_hi), slab: 32 (over y, z_lo, core).
Axes of the slice: x: 4, y: 4, z: 8 (z_hi: 2, z_lo: 4; z = z_hi * 4 + z_lo), core: 2. Of those that a mesh axis runs over, the one named last changes fastest.
Arguments:
- prior_ensemble_fields: float32 [64, 6, 256, 1, 1024], P('member', None, 'slab'), may hold values from -6 to 6
- params: float32 [64, 12], P('member'), may hold values from -3 to 3
- influence: int32 [12, 6], replicated, may hold values 0 or 1
- obs_cell: int32 [256, 8, 128], P('slab', 'member'), may hold values from 0 to 767
- obs_value: float32 [256, 8, 128], P('slab', 'member'), may hold values from -6 to 6
- obs_prec: float32 [256, 8, 128], P('slab', 'member'), may hold values from 0.5 to 4
- cutoff: int32 [256], P('slab'), may hold values from 4 to 8, as said below
Outputs:
- analysis: bfloat16 [64, 6, 256, 1, 1024], P('member', None, 'slab')
- param_analysis: float32 [64, 12], P('member')
Inputs may be any that keep to these rules, and one draw needn't show every extreme that they name: `obs_cell`: index = field * 128 + level * 128 + column within the block. `cutoff`: 8 is reached by some rows.
All inputs are finite; a program needn't handle non-finite values.
Results may differ from a plain program's by a relative error of at most 0.0056.
Values may be sent and summed in bfloat16 or wider, within the bound.
A program may use at most 64 MiB of HBM per device.

v0:
```python
import math

import jax
import jax.numpy as jnp
from jax import lax
from jax.experimental import pallas as pl
from jax.experimental.pallas import tpu as pltpu
from jax.sharding import PartitionSpec as P

STEPS = 4
HALO = 8
NS_STEPS = 5
MESH = pl.DeviceIdType.MESH
F32 = jnp.float32
BF16 = jnp.bfloat16

diffusion = 0.2
advection = 0.15
vertical = 0.1
coupling = 0.2

M = 8
F = 6
R = 8
T = 8
LANES = 128
ENS = 64
W = STEPS


def split(a):
    high = a.astype(BF16)
    return high, (a - high.astype(F32)).astype(BF16)


def dot(a, b):
    return jnp.dot(a, b, preferred_element_type=F32)


def dot_nt(a, b):
    return lax.dot_general(a, b, (((1,), (1,)), ((), ())), preferred_element_type=F32)


def mm(left, right):
    lh, ll = split(left)
    rh, rl = split(right)
    return dot(lh, rh) + (dot(lh, rl) + dot(ll, rh))


def mm_nt(left, right):
    lh, ll = split(left)
    rh, rl = split(right)
    return dot_nt(lh, rh) + (dot_nt(lh, rl) + dot_nt(ll, rh))


def kernel(
    slabs,
    group,
    x_ref, params_ref, infl_ref, cell_ref, value_ref, prec_ref, cut_ref,
    out_ref, pout_ref,
    s0, s1, s2, s3, hs, hr, xs, xr, ys, yr, oc, pv, pp, gs, am, os_, ps, ra, rb, rc,
    load_sem, halo_send, halo_recv, pv_send, pv_recv, oc_send, oc_recv, pp_send, pp_recv,
    ys_send, ys_recv, yf_send, yf_recv, xs_send, xs_recv, os_send, os_recv,
    ra_send, ra_recv, rb_send, rb_recv, rc_send, rc_recv, own_sem,
):
    mu = lax.axis_index("member")
    sl = lax.axis_index("slab")
    has_low = sl > 0
    has_high = sl < slabs - 1
    bands = slabs // group
    band, place = sl // group, lax.rem(sl, group)

    loads = []
    for f in range(F):
        for m in range(M):
            copy = pltpu.make_async_copy(
                x_ref.at[m, f], s0.at[f, pl.ds(W, R), :, m, :], load_sem.at[f, m]
            )
            copy.start()
            loads.append(copy)

    barrier = pltpu.get_barrier_semaphore()
    others = [lax.rem(mu + i, M) for i in range(M)]
    for i in range(1, M):
        pl.semaphore_signal(barrier, inc=1, device_id=(others[i], sl), device_id_type=MESH)
    for i in range(1, group):
        peer = band * group + lax.rem(place + i, group)
        pl.semaphore_signal(barrier, inc=1, device_id=(mu, peer), device_id_type=MESH)
    for i in range(1, bands):
        peer = lax.rem(sl + i * group, slabs)
        pl.semaphore_signal(barrier, inc=1, device_id=(mu, peer), device_id_type=MESH)

    @pl.when(has_low)
    def _():
        pl.semaphore_signal(barrier, inc=1, device_id=(mu, sl - 1), device_id_type=MESH)

    @pl.when(has_high)
    def _():
        pl.semaphore_signal(barrier, inc=1, device_id=(mu, sl + 1), device_id_type=MESH)

    expected = (M - 1) + (group - 1) + (bands - 1)
    expected = expected + jnp.where(has_low, 1, 0) + jnp.where(has_high, 1, 0)
    pl.semaphore_wait(barrier, expected)

    def halo_copy(side, f):
        peer = sl - 1 if side == 0 else sl + 1
        return pltpu.make_async_remote_copy(
            src_ref=hs.at[side, f], dst_ref=hr.at[1 - side, f],
            send_sem=halo_send.at[side, f], recv_sem=halo_recv.at[1 - side, f],
            device_id=(mu, peer), device_id_type=MESH,
        )

    for f in range(F):
        for m in range(M):
            loads[f * M + m].wait()
        for side in range(2):
            for q in range(2):
                row = W + 4 * side + 2 * q
                pair = jnp.concatenate([s0[f, row], s0[f, row + 1]], axis=1)
                hs[side, f, q] = pair.astype(BF16)

        @pl.when(has_low)
        def _():
            halo_copy(0, f).start()

        @pl.when(has_high)
        def _():
            halo_copy(1, f).start()

    pp[mu] = jnp.zeros((M, LANES), F32)
    pp[mu, :, : params_ref.shape[1]] = params_ref[...]
    oc[mu] = cell_ref[...]
    pv[0, 0] = prec_ref[...]
    pv[0, 1] = value_ref[...]

    def pp_copy(i):
        return pltpu.make_async_remote_copy(
            src_ref=pp.at[mu], dst_ref=pp.at[mu], send_sem=pp_send.at[i], recv_sem=pp_recv.at[i],
            device_id=(others[i], sl), device_id_type=MESH,
        )

    def oc_copy(i):
        return pltpu.make_async_remote_copy(
            src_ref=oc.at[mu], dst_ref=oc.at[mu], send_sem=oc_send.at[i], recv_sem=oc_recv.at[i],
            device_id=(others[i], sl), device_id_type=MESH,
        )

    def pv_copy(side):
        peer = sl - 1 if side == 0 else sl + 1
        return pltpu.make_async_remote_copy(
            src_ref=pv.at[0], dst_ref=pv.at[2 - side], send_sem=pv_send.at[side], recv_sem=pv_recv.at[1 - side],
            device_id=(mu, peer), device_id_type=MESH,
        )

    for i in range(1, M):
        oc_copy(i).start()
        pp_copy(i).start()

    @pl.when(has_low)
    def _():
        pv_copy(0).start()

    @pl.when(has_high)
    def _():
        pv_copy(1).start()

    coef = lax.dot_general(
        params_ref[...], infl_ref[...].astype(F32), (((1,), (1,)), ((), ())),
        precision=lax.Precision.HIGHEST, preferred_element_type=F32,
    )
    pull = [jnp.broadcast_to(coupling * coef[:, f : f + 1], (M, LANES))[None] for f in range(F)]
    lane = lax.broadcasted_iota(jnp.int32, (T, M, LANES), 2)
    first, last = lane == 0, lane == LANES - 1
    below = vertical
    centre = (1.0 - 4.0 * diffusion - vertical) + below

    def advance(src, row, f, tile, after):
        rolled = pltpu.roll(tile, LANES - 1, 2)
        right = jnp.where(last, jnp.concatenate([rolled[1:], rolled[:1]], axis=0), rolled)
        rolled = pltpu.roll(tile, 1, 2)
        left = jnp.where(first, jnp.concatenate([rolled[-1:], rolled[:-1]], axis=0), rolled)
        return (
            centre * tile
            + diffusion * (src[f, row + 1] + src[f, row - 1])
            + (diffusion - advection) * right
            + (diffusion + advection) * left
            + pull[f] * after
        )

    def rows_on(src, dst, start, count, edge):
        def body(k, carry):
            row = start + k
            if edge:
                y = sl * R + row - W
                keep = jnp.where((y >= 0) & (y < slabs * R), 1.0, 0.0).astype(F32)
            tile = src[0, row]
            head = tile
            for f in range(F):
                after = src[f + 1, row] if f + 1 < F else head
                new = advance(src, row, f, tile, after)
                dst[f, row] = new * keep if edge else new
                tile = after
            return carry

        lax.fori_loop(0, count, body, 0)

    rows_on(s0, s1, W + 1, R - 2, False)
    rows_on(s1, s2, W + 2, R - 4, False)
    rows_on(s2, s3, W + 3, R - 6, False)

    for side in range(2):
        there = has_low if side == 0 else has_high
        base = 0 if side == 0 else W + R

        @pl.when(there)
        def _():
            for f in range(F):
                pltpu.make_async_remote_copy(
                    src_ref=hs.at[1 - side, f], dst_ref=hr.at[side, f],
                    send_sem=halo_send.at[1 - side, f], recv_sem=halo_recv.at[side, f],
                    device_id=(mu, sl), device_id_type=MESH,
                ).wait_recv()
                for q in range(2):
                    pair = hr[side, f, q].astype(F32)
                    s0[f, base + 2 * q] = pair[:, :M]
                    s0[f, base + 2 * q + 1] = pair[:, M:]

        @pl.when(jnp.logical_not(there))
        def _():
            for f in range(F):
                for k in range(W):
                    s0[f, base + k] = jnp.zeros((T, M, LANES), F32)

    rows_on(s0, s1, 1, 4, True)
    rows_on(s0, s1, 11, 4, True)
    rows_on(s1, s2, 2, 4, True)
    rows_on(s1, s2, 10, 4, True)
    rows_on(s2, s3, 3, 4, True)
    rows_on(s2, s3, 9, 4, True)

    def last_step(q, carry):
        row = W + 2 * q
        tiles = [s3[0, row], s3[0, row + 1]]
        heads = tiles
        for f in range(F):
            afters = [s3[f + 1, row], s3[f + 1, row + 1]] if f + 1 < F else heads
            new = [advance(s3, row + k, f, tiles[k], afters[k]) for k in range(2)]
            xs[f, :, pl.ds(pl.multiple_of(q * 2 * M, 2 * M), 2 * M), :] = jnp.concatenate(new, axis=1).astype(BF16)
            tiles = afters
        return carry

    lax.fori_loop(0, R // 2, last_step, 0)

    for i in range(1, M):
        oc_copy(i).wait()

    def observe(q, carry):
        at = pl.ds(pl.multiple_of(q * 2 * M, 2 * M), 2 * M)
        cells = [jnp.broadcast_to(oc[:, pl.ds(2 * q + k, 1), :], (T, M, LANES)) for k in range(2)]
        cells = jnp.concatenate(cells, axis=1).reshape(T * 2 * M, LANES)
        kind, column = cells // LANES, lax.rem(cells, LANES)
        seen = jnp.zeros((T * 2 * M, LANES), F32)
        for f in range(F):
            tile = xs[f, :, at, :].astype(F32).reshape(T * 2 * M, LANES)
            picked = jnp.take_along_axis(tile, column, axis=1, mode="promise_in_bounds")
            seen = jnp.where(kind == f, picked, seen)
        ys[:, at, :] = seen.reshape(T, 2 * M, LANES).astype(BF16)
        return carry

    lax.fori_loop(0, R // 2, observe, 0)

    def ys_copy(i):
        return pltpu.make_async_remote_copy(
            src_ref=ys.at[others[i]], dst_ref=yr.at[0, mu], send_sem=ys_send.at[i], recv_sem=ys_recv.at[i],
            device_id=(others[i], sl), device_id_type=MESH,
        )

    def xs_copy(f, i):
        return pltpu.make_async_remote_copy(
            src_ref=xs.at[f, others[i]], dst_ref=xr.at[f, mu], send_sem=xs_send.at[f, i], recv_sem=xs_recv.at[f, i],
            device_id=(others[i], sl), device_id_type=MESH,
        )

    for i in range(1, M):
        ys_copy(i).start()
    own_y = pltpu.make_async_copy(ys.at[mu], yr.at[0, mu], own_sem.at[0])
    own_y.start()
    own_x = pltpu.make_async_copy(xs.at[:, mu], xr.at[:, mu], own_sem.at[1])
    own_x.start()
    for f in range(F):
        for i in range(1, M):
            xs_copy(f, i).start()

    def yf_copy(side, i):
        peer = sl - 1 if side == 0 else sl + 1
        origin = lax.rem(mu - i + M, M)
        return pltpu.make_async_remote_copy(
            src_ref=yr.at[0, origin], dst_ref=yr.at[2 - side, origin],
            send_sem=yf_send.at[side, i], recv_sem=yf_recv.at[1 - side, i],
            device_id=(mu, peer), device_id_type=MESH,
        )

    for i in range(M):
        if i == 0:
            own_y.wait()
        else:
            ys_copy(i).wait()

        @pl.when(has_low)
        def _():
            yf_copy(0, i).start()

        @pl.when(has_high)
        def _():
            yf_copy(1, i).start()

    def gram_rows(slot):
        first_row = (R, 0, 2 * R)[slot]

        def body(q, carry):
            at = pl.ds(pl.multiple_of(q * 2 * M, 2 * M), 2 * M)
            pair = yr[slot, :, at, :].astype(F32)
            for k in range(2):
                y = pair[:, k * M : (k + 1) * M, :].reshape(ENS, LANES)
                mean = jnp.sum(y, axis=0, keepdims=True) * (1.0 / ENS)
                pert = y - mean
                prec = pv[slot, 0, pl.ds(2 * q + k, 1), :]
                value = pv[slot, 1, pl.ds(2 * q + k, 1), :]
                weighted = jnp.broadcast_to(prec * (value - mean), (8, LANES))
                left = jnp.concatenate([pert * prec, weighted], axis=0)
                gs[first_row + 2 * q + k] = mm_nt(left, jnp.concatenate([pert, pert], axis=0))
            return carry

        lax.fori_loop(0, R // 2, body, 0)

    gram_rows(0)
    for side in range(2):
        there = has_low if side == 0 else has_high

        @pl.when(there)
        def _():
            pltpu.make_async_remote_copy(
                src_ref=pv.at[0], dst_ref=pv.at[1 + side], send_sem=pv_send.at[1 - side], recv_sem=pv_recv.at[side],
                device_id=(mu, sl), device_id_type=MESH,
            ).wait_recv()
            for i in range(M):
                origin = lax.rem(mu - i + M, M)
                pltpu.make_async_remote_copy(
                    src_ref=yr.at[0, origin], dst_ref=yr.at[1 + side, origin],
                    send_sem=yf_send.at[1 - side, i], recv_sem=yf_recv.at[side, i],
                    device_id=(mu, sl), device_id_type=MESH,
                ).wait_recv()

        @pl.when(jnp.logical_not(there))
        def _():
            yr[1 + side] = jnp.zeros((M, R * M, LANES), BF16)
            pv[1 + side] = jnp.zeros((2, R, LANES), F32)

        gram_rows(1 + side)

    row64 = lax.broadcasted_iota(jnp.int32, (ENS, LANES), 0)
    lane64 = lax.broadcasted_iota(jnp.int32, (ENS, LANES), 1)
    low64 = lane64 < ENS
    eye = jnp.where(lax.rem(lane64, ENS) == row64, 1.0, 0.0).astype(F32)
    y18 = lax.broadcasted_iota(jnp.int32, (24, LANES), 0)
    low18 = lax.broadcasted_iota(jnp.int32, (24, LANES), 1) < ENS
    low1 = low18[:1]

    def both(a):
        return jnp.concatenate([jnp.where(low64, a, 0.0), jnp.where(low64, 0.0, a)], axis=0)

    amats, gvecs, scales = [], [], []
    for p in range(R // 2):
        radius = jnp.where(low18, cut_ref[2 * p], cut_ref[2 * p + 1]).astype(F32)
        away = jnp.abs(y18 - jnp.where(low18, 2 * p + R, 2 * p + 1 + R)).astype(F32)
        weight = jnp.maximum(0.0, 1.0 - away / (radius + 1.0))
        total = jnp.zeros((ENS + 8, LANES), F32)
        for y in range(2 * p, 2 * p + 2 * HALO + 2):
            total = total + weight[y : y + 1] * gs[y]
        amat = (ENS - 1.0) * eye + total[:ENS]
        sums = jnp.sum(amat * amat, axis=0, keepdims=True)
        low = jnp.sum(jnp.where(low1, sums, 0.0), axis=1, keepdims=True)
        high = jnp.sum(jnp.where(low1, 0.0, sums), axis=1, keepdims=True)
        amats.append(amat)
        gvecs.append(total[ENS:])
        scales.append(jnp.sqrt(jnp.where(low1, low, high)))

    ymats = [a / s for a, s in zip(amats, scales)]
    middles = [1.5 * eye - 0.5 * y for y in ymats]
    zmats = middles
    ymats = [mm(y, both(m)) for y, m in zip(ymats, middles)]
    for step_idx in range(1, NS_STEPS):
        middles = [1.5 * eye - 0.5 * mm(z, both(y)) for z, y in zip(zmats, ymats)]
        if step_idx + 1 < NS_STEPS:
            new = [mm(jnp.concatenate([y, z], axis=0), both(m)) for y, z, m in zip(ymats, zmats, middles)]
            ymats, zmats = [n[:ENS] for n in new], [n[ENS:] for n in new]
        else:
            zmats = [mm(m, both(z)) for m, z in zip(middles, zmats)]

    source = lax.broadcasted_iota(jnp.int32, (LANES, LANES), 0)
    target = lax.broadcasted_iota(jnp.int32, (LANES, LANES), 1)
    same_row = source // ENS == lax.rem(target // M, 2)
    same_member = lax.rem(source, ENS) == (target // (2 * M)) * M + lax.rem(target, M)
    spread = jnp.where(same_row, jnp.where(same_member, 1.0 - 1.0 / ENS, -1.0 / ENS), 0.0).astype(BF16)
    odd64 = lax.rem(lane64 // M, 2) == 1
    am[...] = jnp.zeros(am.shape, F32)
    vsum = jnp.zeros((ENS, LANES), F32)
    for p in range(R // 2):
        z, scale = both(zmats[p]), scales[p]
        wbar = mm(mm(gvecs[p], z), z)[:1] / scale
        v = math.sqrt(ENS - 1.0) * zmats[p] / jnp.sqrt(scale) + wbar
        vsum = vsum + v
        vh, vl = split(v)
        a = dot(vh, spread) + dot(vl, spread) + 1.0 / ENS
        am[p, pl.ds(2 * p, ENS, stride=R), :] = jnp.where(odd64, 0.0, a)
        am[p, pl.ds(2 * p + 1, ENS, stride=R), :] = jnp.where(odd64, a, 0.0)

    for i in range(1, M):
        pp_copy(i).wait()
    every = pp[...].reshape(ENS, LANES)
    pbar = jnp.sum(every, axis=0, keepdims=True) * (1.0 / ENS)
    ppert = every - pbar
    ps[...] = mm(vsum, jnp.concatenate([ppert, ppert], axis=0)).reshape(M, M, LANES)

    def ra_copy(i):
        return pltpu.make_async_remote_copy(
            src_ref=ps.at[others[i]], dst_ref=ra.at[mu], send_sem=ra_send.at[i], recv_sem=ra_recv.at[i],
            device_id=(others[i], sl), device_id_type=MESH,
        )

    for i in range(1, M):
        ra_copy(i).start()
    ra[mu] = ps[mu]

    lanes_here = pl.ds(pl.multiple_of(mu * LANES, LANES), LANES)

    def os_copy(f, i):
        return pltpu.make_async_remote_copy(
            src_ref=os_.at[f, others[i]], dst_ref=out_ref.at[:, f, :, lanes_here],
            send_sem=os_send.at[f, i], recv_sem=os_recv.at[f, i],
            device_id=(others[i], sl), device_id_type=MESH,
        )

    def own_copy(f):
        return pltpu.make_async_copy(os_.at[f, mu], out_ref.at[:, f, :, lanes_here], own_sem.at[2 + f])

    own_x.wait()
    for f in range(F):
        for i in range(1, M):
            xs_copy(f, i).wait()
        tiles = [xr[f, :, q * 2 * M : (q + 1) * 2 * M, :].reshape(2 * ENS, LANES) for q in range(R // 2)]
        field = jnp.concatenate(tiles, axis=0)
        for h in range(4):
            ah, al = split(jnp.concatenate([am[p, h * LANES : (h + 1) * LANES, :] for p in range(R // 2)], axis=1))
            new = dot(ah, field) + dot(al, field)
            os_[f, 2 * h : 2 * h + 2] = new.reshape(2, M, R, LANES).astype(BF16)
        for i in range(1, M):
            os_copy(f, i).start()
        own_copy(f).start()

    for i in range(1, M):
        ra_copy(i).wait()
    rb[place] = jnp.sum(ra[...], axis=0)

    def rb_copy(i):
        peer = band * group + lax.rem(place + i, group)
        return pltpu.make_async_remote_copy(
            src_ref=rb.at[place], dst_ref=rb.at[place], send_sem=rb_send.at[i], recv_sem=rb_recv.at[i],
            device_id=(mu, peer), device_id_type=MESH,
        )

    def rc_copy(i):
        peer = lax.rem(sl + i * group, slabs)
        return pltpu.make_async_remote_copy(
            src_ref=rc.at[band], dst_ref=rc.at[band], send_sem=rc_send.at[i], recv_sem=rc_recv.at[i],
            device_id=(mu, peer), device_id_type=MESH,
        )

    for i in range(1, group):
        rb_copy(i).start()
    for i in range(1, group):
        rb_copy(i).wait()
    rc[band] = jnp.sum(rb[...], axis=0)
    for i in range(1, bands):
        rc_copy(i).start()
    for i in range(1, bands):
        rc_copy(i).wait()
    total = jnp.sum(rc[...], axis=0) * (1.0 / (slabs * R * M)) + pbar
    pout_ref[...] = total[:, : pout_ref.shape[1]]

    for f in range(F):
        for i in range(1, M):
            os_copy(f, i).wait()
        own_copy(f).wait()
    for side in range(2):
        there = has_low if side == 0 else has_high

        @pl.when(there)
        def _():
            for f in range(F):
                halo_copy(side, f).wait_send()
            pv_copy(side).wait_send()
            for i in range(M):
                yf_copy(side, i).wait_send()


def local(prior_ensemble_fields, params, influence, obs_cell, obs_value, obs_prec, cutoff):
    slabs = lax.axis_size("slab")
    group = 8 if slabs % 8 == 0 else slabs
    bands = slabs // group
    npar = params.shape[1]
    vmem = pl.BlockSpec(memory_space=pltpu.VMEM)
    dma = pltpu.SemaphoreType.DMA
    ext = R + 2 * W
    analysis, param_analysis = pl.pallas_call(
        lambda *refs: kernel(slabs, group, *refs),
        out_shape=(
            jax.ShapeDtypeStruct((M, F, R, T * LANES), BF16),
            jax.ShapeDtypeStruct((M, npar), F32),
        ),
        in_specs=[
            pl.BlockSpec(memory_space=pl.ANY), vmem, vmem, vmem, vmem, vmem,
            pl.BlockSpec(memory_space=pltpu.SMEM),
        ],
        out_specs=(pl.BlockSpec(memory_space=pl.ANY), vmem),
        scratch_shapes=[
            pltpu.VMEM((F, ext, T, M, LANES), F32),
            pltpu.VMEM((F, ext, T, M, LANES), F32),
            pltpu.VMEM((F, ext, T, M, LANES), F32),
            pltpu.VMEM((F, ext, T, M, LANES), F32),
            pltpu.VMEM((2, F, 2, T, 2 * M, LANES), BF16),
            pltpu.VMEM((2, F, 2, T, 2 * M, LANES), BF16),
            pltpu.VMEM((F, T, R * M, LANES), BF16),
            pltpu.VMEM((F, M, R * M, LANES), BF16),
            pltpu.VMEM((T, R * M, LANES), BF16),
            pltpu.VMEM((3, M, R * M, LANES), BF16),
            pltpu.VMEM((M, R, LANES), jnp.int32),
            pltpu.VMEM((3, 2, R, LANES), F32),
            pltpu.VMEM((M, M, LANES), F32),
            pltpu.VMEM((3 * R, ENS + 8, LANES), F32),
            pltpu.VMEM((R // 2, ENS * R, LANES), F32),
            pltpu.VMEM((F, M, M, R, LANES), BF16),
            pltpu.VMEM((M, M, LANES), F32),
            pltpu.VMEM((M, M, LANES), F32),
            pltpu.VMEM((group, M, LANES), F32),
            pltpu.VMEM((bands, M, LANES), F32),
            dma((F, M)), dma((2, F)), dma((2, F)), dma((2,)), dma((2,)),
            dma((M,)), dma((M,)), dma((M,)), dma((M,)),
            dma((M,)), dma((M,)), dma((2, M)), dma((2, M)), dma((F, M)), dma((F, M)), dma((F, M)), dma((F, M)),
            dma((M,)), dma((M,)), dma((group,)), dma((group,)), dma((bands,)), dma((bands,)), dma((2 + F,)),
        ],
        compiler_params=pltpu.CompilerParams(
            collective_id=0, has_side_effects=True, vmem_limit_bytes=56 * 1024 * 1024
        ),
        name="cycle",
    )(
        prior_ensemble_fields.reshape(M, F, R, T, LANES),
        params,
        influence.T,
        obs_cell.reshape(R, LANES),
        obs_value.reshape(R, LANES),
        obs_prec.reshape(R, LANES),
        cutoff,
    )
    return analysis.reshape(M, F, R, 1, T * LANES), param_analysis


def solution(mesh):
    in_specs = (
        P("member", None, "slab", None, None),
        P("member", None),
        P(),
        P("slab", "member", None),
        P("slab", "member", None),
        P("slab", "member", None),
        P("slab"),
    )
    out_specs = (P("member", None, "slab", None, None), P("member", None))
    return jax.shard_map(local, mesh=mesh, in_specs=in_specs, out_specs=out_specs, check_vma=False)
```

profile of v0, /device:TPU:1, one launch (start us, length us, event | category | flops | bytes accessed | tf_op | source)
XLA Modules:
  0.0 86.4 jit_solution(13390563139328548835)
XLA Ops:
  0.6 83.1 %cycle.1 = (bf16[8,6,8,1024]{3,2,1,0:T(8,128)(2,1)}, f32[8,12]{1,0:T(8,128)}) custom-call(f32[8,6,8,8,128]{4,3,2,1,0:T(8,128)} %bitcast.8, f32[8,12]{1,0:T(8,128)} %refs_1_.1, s32[6,12]{1,0:T(8,128)} %bitcast.10, s32[8,128]{1,0:T(8,128)} %bitcast.11, f32[8,128]{1,0:T(8,128)} %bitcast.12, f32[8,128]{1,0:T(8,128)} %bitcast.13, s32[8]{0:T(128)} %refs_6_.1), custom_call_target="tpu_custom_call" | custom-call | tf_op jit(solution)/shard_map/cycle/pallas_call | solution.py:515
  83.7 0.0 copy-start
  83.7 2.1 %copy.12 = bf16[8,6,8,1,1024]{4,2,3,1,0:T(8,128)(2,1)} copy(bf16[8,6,8,1,1024]{4,2,3,1,0:T(8,128)(2,1)} %bitcast.9) | data formatting | bytes 1572864
  85.8 0.0 copy-done
  85.8 0.6 copy.13
Async XLA Ops:
  83.7 2.1 %copy-start = (f32[8,12]{1,0:T(8,128)S(1)}, f32[8,12]{1,0:T(8,128)}, u32[]{:S(2)}) copy-start(f32[8,12]{1,0:T(8,128)} %get-tuple-element.11) | copy-start | bytes 1156
where the time goes:
time: 86.5 us; the launch traced here: 86.4 us
  Pallas kernels  83.1 us (96%)
  local copies, waits for them, and re-layouts  2.66 us (3%)
    pallas_call x1, Pallas kernels, local(): pl.pallas_call(lambda *refs: kernel(slabs, group, *refs), out_shape=(jax....  83.1 us
    unnamed x4, local copies, waits for them, and re-layouts  2.66 us

commit v1 on v0

--- a/solution.py
+++ b/solution.py
@@ -9,6 +9,8 @@
 
 STEPS = 4
 HALO = 8
+EARLY = 3
+STAGE_AT = (5, 5)
 NS_STEPS = 5
 MESH = pl.DeviceIdType.MESH
 F32 = jnp.float32
@@ -208,36 +210,6 @@
     rows_on(s1, s2, W + 2, R - 4, False)
     rows_on(s2, s3, W + 3, R - 6, False)
 
-    for side in range(2):
-        there = has_low if side == 0 else has_high
-        base = 0 if side == 0 else W + R
-
-        @pl.when(there)
-        def _():
-            for f in range(F):
-                pltpu.make_async_remote_copy(
-                    src_ref=hs.at[1 - side, f], dst_ref=hr.at[side, f],
-                    send_sem=halo_send.at[1 - side, f], recv_sem=halo_recv.at[side, f],
-                    device_id=(mu, sl), device_id_type=MESH,
-                ).wait_recv()
-                for q in range(2):
-                    pair = hr[side, f, q].astype(F32)
-                    s0[f, base + 2 * q] = pair[:, :M]
-                    s0[f, base + 2 * q + 1] = pair[:, M:]
-
-        @pl.when(jnp.logical_not(there))
-        def _():
-            for f in range(F):
-                for k in range(W):
-                    s0[f, base + k] = jnp.zeros((T, M, LANES), F32)
-
-    rows_on(s0, s1, 1, 4, True)
-    rows_on(s0, s1, 11, 4, True)
-    rows_on(s1, s2, 2, 4, True)
-    rows_on(s1, s2, 10, 4, True)
-    rows_on(s2, s3, 3, 4, True)
-    rows_on(s2, s3, 9, 4, True)
-
     def last_step(q, carry):
         row = W + 2 * q
         tiles = [s3[0, row], s3[0, row + 1]]
@@ -249,10 +221,6 @@
             tiles = afters
         return carry
 
-    lax.fori_loop(0, R // 2, last_step, 0)
-
-    for i in range(1, M):
-        oc_copy(i).wait()
 
     def observe(q, carry):
         at = pl.ds(pl.multiple_of(q * 2 * M, 2 * M), 2 * M)
@@ -267,7 +235,39 @@
         ys[:, at, :] = seen.reshape(T, 2 * M, LANES).astype(BF16)
         return carry
 
-    lax.fori_loop(0, R // 2, observe, 0)
+    near = 1 - lax.rem(sl, 2)
+    for order in range(2):
+        side = near if order == 0 else 1 - near
+        there = jnp.where(side == 0, sl, slabs - 1 - sl) > 0
+        base = side * (W + R)
+
+        @pl.when(there)
+        def _():
+            for f in range(F):
+                pltpu.make_async_remote_copy(
+                    src_ref=hs.at[1 - side, f], dst_ref=hr.at[side, f],
+                    send_sem=halo_send.at[1 - side, f], recv_sem=halo_recv.at[side, f],
+                    device_id=(mu, sl), device_id_type=MESH,
+                ).wait_recv()
+                for q in range(2):
+                    pair = hr[side, f, q].astype(F32)
+                    s0[f, base + 2 * q] = pair[:, :M]
+                    s0[f, base + 2 * q + 1] = pair[:, M:]
+
+        @pl.when(jnp.logical_not(there))
+        def _():
+            for f in range(F):
+                for k in range(W):
+                    s0[f, base + k] = jnp.zeros((T, M, LANES), F32)
+
+        rows_on(s0, s1, 1 + 10 * side, 4, True)
+        rows_on(s1, s2, 2 + 8 * side, 4, True)
+        rows_on(s2, s3, 3 + 6 * side, 4, True)
+        lax.fori_loop(2 * side, 2 * side + 2, last_step, 0)
+        if order == 0:
+            for i in range(1, M):
+                oc_copy(i).wait()
+        lax.fori_loop(2 * side, 2 * side + 2, observe, 0)
 
     def ys_copy(i):
         return pltpu.make_async_remote_copy(
@@ -287,7 +287,7 @@
     own_y.start()
     own_x = pltpu.make_async_copy(xs.at[:, mu], xr.at[:, mu], own_sem.at[1])
     own_x.start()
-    for f in range(F):
+    for f in range(EARLY):
         for i in range(1, M):
             xs_copy(f, i).start()
 
@@ -313,6 +313,10 @@
         @pl.when(has_high)
         def _():
             yf_copy(1, i).start()
+
+    for f in range(EARLY, F):
+        for i in range(1, M):
+            xs_copy(f, i).start()
 
     def gram_rows(slot):
         first_row = (R, 0, 2 * R)[slot]
@@ -444,6 +448,20 @@
     def own_copy(f):
         return pltpu.make_async_copy(os_.at[f, mu], out_ref.at[:, f, :, lanes_here], own_sem.at[2 + f])
 
+    def rb_copy(i):
+        peer = band * group + lax.rem(place + i, group)
+        return pltpu.make_async_remote_copy(
+            src_ref=rb.at[place], dst_ref=rb.at[place], send_sem=rb_send.at[i], recv_sem=rb_recv.at[i],
+            device_id=(mu, peer), device_id_type=MESH,
+        )
+
+    def rc_copy(i):
+        peer = lax.rem(sl + i * group, slabs)
+        return pltpu.make_async_remote_copy(
+            src_ref=rc.at[band], dst_ref=rc.at[band], send_sem=rc_send.at[i], recv_sem=rc_recv.at[i],
+            device_id=(mu, peer), device_id_type=MESH,
+        )
+
     own_x.wait()
     for f in range(F):
         for i in range(1, M):
@@ -458,31 +476,19 @@
             os_copy(f, i).start()
         own_copy(f).start()
 
-    for i in range(1, M):
-        ra_copy(i).wait()
-    rb[place] = jnp.sum(ra[...], axis=0)
-
-    def rb_copy(i):
-        peer = band * group + lax.rem(place + i, group)
-        return pltpu.make_async_remote_copy(
-            src_ref=rb.at[place], dst_ref=rb.at[place], send_sem=rb_send.at[i], recv_sem=rb_recv.at[i],
-            device_id=(mu, peer), device_id_type=MESH,
-        )
-
-    def rc_copy(i):
-        peer = lax.rem(sl + i * group, slabs)
-        return pltpu.make_async_remote_copy(
-            src_ref=rc.at[band], dst_ref=rc.at[band], send_sem=rc_send.at[i], recv_sem=rc_recv.at[i],
-            device_id=(mu, peer), device_id_type=MESH,
-        )
-
-    for i in range(1, group):
-        rb_copy(i).start()
-    for i in range(1, group):
-        rb_copy(i).wait()
-    rc[band] = jnp.sum(rb[...], axis=0)
-    for i in range(1, bands):
-        rc_copy(i).start()
+        if f == STAGE_AT[0]:
+            for i in range(1, M):
+                ra_copy(i).wait()
+            rb[place] = jnp.sum(ra[...], axis=0)
+            for i in range(1, group):
+                rb_copy(i).start()
+        if f == STAGE_AT[1]:
+            for i in range(1, group):
+                rb_copy(i).wait()
+            rc[band] = jnp.sum(rb[...], axis=0)
+            for i in range(1, bands):
+                rc_copy(i).start()
+
     for i in range(1, bands):
         rc_copy(i).wait()
     total = jnp.sum(rc[...], axis=0) * (1.0 / (slabs * R * M)) + pbar

time: 86.5 us -> 80.4 us (0.929)
  Pallas kernels: 83.1 us -> 77 us
    pallas_call x1, Pallas kernels: 83.1 us -> 77 us  [local(): pl.pallas_call(lambda *refs: kernel(slabs, group, *refs), out_shape=(jax....]
where the time goes in v1:
time: 80.4 us; the launch traced here: 80.3 us
  Pallas kernels  77 us (96%)
  local copies, waits for them, and re-layouts  2.66 us (3%)
    pallas_call x1, Pallas kernels, local(): pl.pallas_call(lambda *refs: kernel(slabs, group, *refs), out_shape=(jax....  77 us
    unnamed x4, local copies, waits for them, and re-layouts  2.66 us

profile of v1, /device:TPU:1, one launch (start us, length us, event | category | flops | bytes accessed | tf_op | source)
XLA Modules:
  0.0 80.3 jit_solution(14131145816922565743)
XLA Ops:
  0.6 77.0 %cycle.1 = (bf16[8,6,8,1024]{3,2,1,0:T(8,128)(2,1)}, f32[8,12]{1,0:T(8,128)}) custom-call(f32[8,6,8,8,128]{4,3,2,1,0:T(8,128)} %bitcast.8, f32[8,12]{1,0:T(8,128)} %refs_1_.1, s32[6,12]{1,0:T(8,128)} %bitcast.10, s32[8,128]{1,0:T(8,128)} %bitcast.11, f32[8,128]{1,0:T(8,128)} %bitcast.12, f32[8,128]{1,0:T(8,128)} %bitcast.13, s32[8]{0:T(128)} %refs_6_.1), custom_call_target="tpu_custom_call" | custom-call | tf_op jit(solution)/shard_map/cycle/pallas_call | solution.py:521
  77.6 0.0 copy-start
  77.6 2.1 %copy.12 = bf16[8,6,8,1,1024]{4,2,3,1,0:T(8,128)(2,1)} copy(bf16[8,6,8,1,1024]{4,2,3,1,0:T(8,128)(2,1)} %bitcast.9) | data formatting | bytes 1572864
  79.7 0.0 copy-done
  79.7 0.6 copy.13
Async XLA Ops:
  77.6 2.1 %copy-start = (f32[8,12]{1,0:T(8,128)S(1)}, f32[8,12]{1,0:T(8,128)}, u32[]{:S(2)}) copy-start(f32[8,12]{1,0:T(8,128)} %get-tuple-element.11) | copy-start | bytes 1156

commit v2 on v1

--- a/solution.py
+++ b/solution.py
@@ -9,8 +9,8 @@
 
 STEPS = 4
 HALO = 8
-EARLY = 3
-STAGE_AT = (5, 5)
+GROUP = 3
+STAGE_AT = (4, 5)
 NS_STEPS = 5
 MESH = pl.DeviceIdType.MESH
 F32 = jnp.float32
@@ -72,15 +72,6 @@
     bands = slabs // group
     band, place = sl // group, lax.rem(sl, group)
 
-    loads = []
-    for f in range(F):
-        for m in range(M):
-            copy = pltpu.make_async_copy(
-                x_ref.at[m, f], s0.at[f, pl.ds(W, R), :, m, :], load_sem.at[f, m]
-            )
-            copy.start()
-            loads.append(copy)
-
     barrier = pltpu.get_barrier_semaphore()
     others = [lax.rem(mu + i, M) for i in range(M)]
     for i in range(1, M):
@@ -102,7 +93,15 @@
 
     expected = (M - 1) + (group - 1) + (bands - 1)
     expected = expected + jnp.where(has_low, 1, 0) + jnp.where(has_high, 1, 0)
-    pl.semaphore_wait(barrier, expected)
+
+    loads = []
+    for f in range(F):
+        for m in range(M):
+            copy = pltpu.make_async_copy(
+                x_ref.at[m, f], s0.at[f, pl.ds(W, R), :, m, :], load_sem.at[f, m]
+            )
+            copy.start()
+            loads.append(copy)
 
     def halo_copy(side, f):
         peer = sl - 1 if side == 0 else sl + 1
@@ -121,6 +120,9 @@
                 pair = jnp.concatenate([s0[f, row], s0[f, row + 1]], axis=1)
                 hs[side, f, q] = pair.astype(BF16)
 
+    pl.semaphore_wait(barrier, expected)
+
+    for f in range(F):
         @pl.when(has_low)
         def _():
             halo_copy(0, f).start()
@@ -276,8 +278,9 @@
         )
 
     def xs_copy(f, i):
-        return pltpu.make_async_remote_copy(
-            src_ref=xs.at[f, others[i]], dst_ref=xr.at[f, mu], send_sem=xs_send.at[f, i], recv_sem=xs_recv.at[f, i],
+        fields = pl.ds(f, GROUP)
+        return pltpu.make_async_remote_copy(
+            src_ref=xs.at[fields, others[i]], dst_ref=xr.at[fields, mu], send_sem=xs_send.at[f, i], recv_sem=xs_recv.at[f, i],
             device_id=(others[i], sl), device_id_type=MESH,
         )
 
@@ -287,9 +290,8 @@
     own_y.start()
     own_x = pltpu.make_async_copy(xs.at[:, mu], xr.at[:, mu], own_sem.at[1])
     own_x.start()
-    for f in range(EARLY):
-        for i in range(1, M):
-            xs_copy(f, i).start()
+    for i in range(1, M):
+        xs_copy(0, i).start()
 
     def yf_copy(side, i):
         peer = sl - 1 if side == 0 else sl + 1
@@ -314,7 +316,7 @@
         def _():
             yf_copy(1, i).start()
 
-    for f in range(EARLY, F):
+    for f in range(GROUP, F, GROUP):
         for i in range(1, M):
             xs_copy(f, i).start()
 
@@ -464,8 +466,9 @@
 
     own_x.wait()
     for f in range(F):
-        for i in range(1, M):
-            xs_copy(f, i).wait()
+        if f % GROUP == 0:
+            for i in range(1, M):
+                xs_copy(f, i).wait()
         tiles = [xr[f, :, q * 2 * M : (q + 1) * 2 * M, :].reshape(2 * ENS, LANES) for q in range(R // 2)]
         field = jnp.concatenate(tiles, axis=0)
         for h in range(4):
@@ -521,14 +524,14 @@
     analysis, param_analysis = pl.pallas_call(
         lambda *refs: kernel(slabs, group, *refs),
         out_shape=(
-            jax.ShapeDtypeStruct((M, F, R, T * LANES), BF16),
-            jax.ShapeDtypeStruct((M, npar), F32),
+            pltpu.VMEM((M, F, R, T * LANES), BF16),
+            pltpu.VMEM((M, npar), F32),
         ),
         in_specs=[
             pl.BlockSpec(memory_space=pl.ANY), vmem, vmem, vmem, vmem, vmem,
             pl.BlockSpec(memory_space=pltpu.SMEM),
         ],
-        out_specs=(pl.BlockSpec(memory_space=pl.ANY), vmem),
+        out_specs=(vmem, vmem),
         scratch_shapes=[
             pltpu.VMEM((F, ext, T, M, LANES), F32),
             pltpu.VMEM((F, ext, T, M, LANES), F32),

time: 80.4 us -> 77.4 us (0.963)
  Pallas kernels: 77 us -> 75.1 us
  local copies, waits for them, and re-layouts: 2.66 us -> 1.47 us
    pallas_call x1, Pallas kernels: 77 us -> 75.1 us  [local(): pl.pallas_call(lambda *refs: kernel(slabs, group, *refs), out_shape=(pltp...]
    unnamed x4 -> x2, local copies, waits for them, and re-layouts: 2.66 us -> 1.47 us
where the time goes in v2:
time: 77.4 us; the launch traced here: 77.2 us
  Pallas kernels  75.1 us (97%)
  local copies, waits for them, and re-layouts  1.47 us (2%)
    pallas_call x1, Pallas kernels, local(): pl.pallas_call(lambda *refs: kernel(slabs, group, *refs), out_shape=(pltp...  75.1 us

profile of v2, /device:TPU:1, one launch (start us, length us, event | category | flops | bytes accessed | tf_op | source)
XLA Modules:
  0.0 77.2 jit_solution(5963529202251847683)
XLA Ops:
  0.6 75.1 %cycle.1 = (bf16[8,6,8,1024]{3,2,1,0:T(8,128)(2,1)S(1)}, f32[8,12]{1,0:T(8,128)S(1)}) custom-call(f32[8,6,8,8,128]{4,3,2,1,0:T(8,128)} %bitcast.9, f32[8,12]{1,0:T(8,128)} %refs_1_.1, s32[6,12]{1,0:T(8,128)} %bitcast.10, s32[8,128]{1,0:T(8,128)} %bitcast.11, f32[8,128]{1,0:T(8,128)} %bitcast.12, f32[8,128]{1,0:T(8,128)} %bitcast.13, s32[8]{0:T(128)} %refs_6_.1), custom_call_target="tpu_custom_call" | custom-call | tf_op jit(solution)/shard_map/cycle/pallas_call | solution.py:524
  75.7 0.9 %copy.12 = bf16[8,6,8,1,1024]{4,2,3,1,0:T(8,128)(2,1)} copy(bf16[8,6,8,1,1024]{4,2,3,1,0:T(8,128)(2,1)S(1)} %bitcast.8) | data formatting | bytes 1572864
  76.6 0.6 copy.13

commit v3 on v2

--- a/solution.py
+++ b/solution.py
@@ -120,6 +120,8 @@
                 pair = jnp.concatenate([s0[f, row], s0[f, row + 1]], axis=1)
                 hs[side, f, q] = pair.astype(BF16)
 
+    am[...] = jnp.zeros(am.shape, F32)
+
     pl.semaphore_wait(barrier, expected)
 
     for f in range(F):
@@ -409,7 +411,6 @@
     same_member = lax.rem(source, ENS) == (target // (2 * M)) * M + lax.rem(target, M)
     spread = jnp.where(same_row, jnp.where(same_member, 1.0 - 1.0 / ENS, -1.0 / ENS), 0.0).astype(BF16)
     odd64 = lax.rem(lane64 // M, 2) == 1
-    am[...] = jnp.zeros(am.shape, F32)
     vsum = jnp.zeros((ENS, LANES), F32)
     for p in range(R // 2):
         z, scale = both(zmats[p]), scales[p]
@@ -421,22 +422,12 @@
         am[p, pl.ds(2 * p, ENS, stride=R), :] = jnp.where(odd64, 0.0, a)
         am[p, pl.ds(2 * p + 1, ENS, stride=R), :] = jnp.where(odd64, a, 0.0)
 
-    for i in range(1, M):
-        pp_copy(i).wait()
-    every = pp[...].reshape(ENS, LANES)
-    pbar = jnp.sum(every, axis=0, keepdims=True) * (1.0 / ENS)
-    ppert = every - pbar
-    ps[...] = mm(vsum, jnp.concatenate([ppert, ppert], axis=0)).reshape(M, M, LANES)
-
     def ra_copy(i):
         return pltpu.make_async_remote_copy(
             src_ref=ps.at[others[i]], dst_ref=ra.at[mu], send_sem=ra_send.at[i], recv_sem=ra_recv.at[i],
             device_id=(others[i], sl), device_id_type=MESH,
         )
 
-    for i in range(1, M):
-        ra_copy(i).start()
-    ra[mu] = ps[mu]
 
     lanes_here = pl.ds(pl.multiple_of(mu * LANES, LANES), LANES)
 
@@ -478,6 +469,16 @@
         for i in range(1, M):
             os_copy(f, i).start()
         own_copy(f).start()
+        if f == 0:
+            for i in range(1, M):
+                pp_copy(i).wait()
+            every = pp[...].reshape(ENS, LANES)
+            pbar = jnp.sum(every, axis=0, keepdims=True) * (1.0 / ENS)
+            ppert = every - pbar
+            ps[...] = mm(vsum, jnp.concatenate([ppert, ppert], axis=0)).reshape(M, M, LANES)
+            for i in range(1, M):
+                ra_copy(i).start()
+            ra[mu] = ps[mu]
 
         if f == STAGE_AT[0]:
             for i in range(1, M):

time: 77.4 us -> 77.4 us (level)
  no operation moved by 1% of the time
where the time goes in v3:
time: 77.4 us; the launch traced here: 77.2 us
  Pallas kernels  75.1 us (97%)
  local copies, waits for them, and re-layouts  1.47 us (2%)
    pallas_call x1, Pallas kernels, local(): pl.pallas_call(lambda *refs: kernel(slabs, group, *refs), out_shape=(pltp...  75.1 us

profile of v3, /device:TPU:1, one launch (start us, length us, event | category | flops | bytes accessed | tf_op | source)
XLA Modules:
  0.0 77.2 jit_solution(2306670825599331)
XLA Ops:
  0.6 75.1 %cycle.1 = (bf16[8,6,8,1024]{3,2,1,0:T(8,128)(2,1)S(1)}, f32[8,12]{1,0:T(8,128)S(1)}) custom-call(f32[8,6,8,8,128]{4,3,2,1,0:T(8,128)} %bitcast.9, f32[8,12]{1,0:T(8,128)} %refs_1_.1, s32[6,12]{1,0:T(8,128)} %bitcast.10, s32[8,128]{1,0:T(8,128)} %bitcast.11, f32[8,128]{1,0:T(8,128)} %bitcast.12, f32[8,128]{1,0:T(8,128)} %bitcast.13, s32[8]{0:T(128)} %refs_6_.1), custom_call_target="tpu_custom_call" | custom-call | tf_op jit(solution)/shard_map/cycle/pallas_call | solution.py:525
  75.7 0.9 %copy.12 = bf16[8,6,8,1,1024]{4,2,3,1,0:T(8,128)(2,1)} copy(bf16[8,6,8,1,1024]{4,2,3,1,0:T(8,128)(2,1)S(1)} %bitcast.8) | data formatting | bytes 1572864
  76.6 0.6 copy.13
